TPU v7x, 32 devices: a whole 2x2x4 slice. The times are simulated.
32 devices in a mesh: gz: 4 (over z), lat: 8 (over y, x, core).
Axes of the slice: x: 2, y: 2, z: 4, core: 2. Of those that a mesh axis runs over, the one named last changes fastest.
Arguments:
- features: bfloat16 [8, 512, 1536], P('lat', 'gz'), may hold values from -6 to 6
- input_map: bfloat16 [8, 512, 128], P('lat', 'gz'), may hold values from -0.5 to 0.5
- output_map: bfloat16 [8, 512, 128], P('lat', 'gz'), may hold values from -0.5 to 0.5
- step_size: float32 [8, 512, 24], P('lat', 'gz'), may hold values from 0.008 to 0.11, as said below
- decay_rate: float32 [24], replicated, may hold values from 0.005859375 to 1, as said below
- skip_gain: float32 [24], replicated, may hold values from 0.5 to 1.5
- kernel: float32 [3, 1536], replicated, may hold values from -2.5 to 2.5
- cotangent: bfloat16 [8, 512, 1536], P(None, ('gz', 'lat')), may hold values from -23 to 23
Outputs:
- lateral_out: bfloat16 [8, 512, 1536], P(None, ('gz', 'lat'))
- grad_features: bfloat16 [8, 512, 1536], P('lat', 'gz')
- grad_input_map: bfloat16 [8, 512, 128], P('lat', 'gz')
- grad_output_map: bfloat16 [8, 512, 128], P('lat', 'gz')
- grad_kernel: float32 [3, 1536], replicated
Inputs may be any that keep to these rules, and one draw needn't show every extreme that they name: `step_size`: positive step sizes. `decay_rate`: positive rates.
All inputs are finite; a program needn't handle non-finite values.
Results may differ from a plain program's by a relative error of at most 0.0069.
Values may be sent and summed in bfloat16 or wider, within the bound.
A program may use at most 128 MiB of HBM per device.

v0:
```python
import math

import jax
import jax.numpy as jnp
from jax import lax
from jax.sharding import PartitionSpec as P


def prefix(part, axis, combine, identity, reverse):
    count = lax.axis_size(axis)
    place = lax.axis_index(axis)
    ahead = count - 1 - place if reverse else place
    gathered = jax.tree.map(lambda a: lax.all_gather(a, axis), part)
    state = jax.tree.map(lambda a, e: jnp.zeros_like(a) + jnp.asarray(e, a.dtype), part, identity)

    def one(step, state):
        source = count - 1 - step if reverse else step
        return combine(
            state, jax.tree.map(lambda a: lax.dynamic_index_in_dim(a, source, 0, False), gathered)
        )

    return lax.fori_loop(0, ahead, one, state)


def decay_head(log_decay, step_head):
    length = log_decay.shape[0]
    row_index = lax.broadcasted_iota(jnp.int32, (length, length), 0)
    col_index = lax.broadcasted_iota(jnp.int32, (length, length), 1)
    spread = log_decay[:, None] - log_decay[None, :]
    return jnp.exp(jnp.where(row_index >= col_index, spread, -jnp.inf)) * step_head[None, :]


def local_terms(input_block, output_block, step_block, decay_rate):
    log_decay = jnp.cumsum(-step_block * decay_rate[None, :], axis=0)
    block_total = log_decay[-1]
    out_weight = step_block * jnp.exp(block_total[None, :] - log_decay)
    map_product = jnp.dot(output_block, input_block.T, preferred_element_type=jnp.float32)
    decay_mask = jax.vmap(decay_head, in_axes=(1, 1))(log_decay, step_block)
    mix_weights = (map_product[None] * decay_mask).astype(jnp.bfloat16)
    in_weights = (input_block.astype(jnp.float32)[:, None, :] * out_weight[:, :, None]).astype(
        jnp.bfloat16
    )
    out_read = (
        output_block.astype(jnp.float32)[:, None, :] * jnp.exp(log_decay)[:, :, None]
    ).astype(jnp.bfloat16)
    return (log_decay, block_total, out_weight, mix_weights, in_weights, out_read)


def chain_combine(earlier, later):
    return (earlier[0] * later[0], later[0][:, :, None, None] * earlier[1] + later[1])


def head_pairs(heads_grad, heads_in, log_decay, step_block):
    length = heads_grad.shape[0]

    def accumulate(summed, pieces):
        grad_head, feat_head, head_log, step_head = pieces
        head_inner = jnp.dot(grad_head, feat_head.T, preferred_element_type=jnp.float32)
        return (summed + head_inner * decay_head(head_log, step_head), None)

    summed, unused = lax.scan(
        accumulate,
        jnp.zeros((length, length), jnp.float32),
        (jnp.swapaxes(heads_grad, 0, 1), jnp.swapaxes(heads_in, 0, 1), log_decay.T, step_block.T),
    )
    return summed.astype(jnp.bfloat16)


def lateral_sum(padded, kernel, extent, flip):
    tap_count = kernel.shape[0]
    summed = 0.0
    for tap_index in range(tap_count):
        anchor = tap_count - 1 - tap_index if flip else tap_index
        summed = summed + kernel[tap_index][None, None, :] * padded[anchor : anchor + extent]
    return summed


def kernel_terms(cotangent, padded, extent):
    tap_count = padded.shape[0] - extent + 1
    return jnp.stack(
        [
            jnp.einsum(
                "xzc,xzc->c",
                cotangent,
                padded[tap_index : tap_index + extent],
                preferred_element_type=jnp.float32,
            )
            for tap_index in range(tap_count)
        ]
    )


def per_device(
    features, input_map, output_map, step_size, decay_rate, skip_gain, kernel, cotangent
):
    columns, sections, channels = features.shape
    head_count = step_size.shape[2]
    head_size = channels // head_count
    state_size = input_map.shape[2]
    log_decay, block_total, out_weight, mix_weights, in_weights, out_read = jax.vmap(
        local_terms, in_axes=(0, 0, 0, None)
    )(input_map, output_map, step_size, decay_rate)
    heads_in = features.reshape(columns, sections, head_count, head_size)
    block_state = jnp.einsum(
        "cihp,cihn->chpn", heads_in, in_weights, preferred_element_type=jnp.float32
    )
    decay_step = jnp.exp(block_total)
    identity = (jnp.ones_like(decay_step), jnp.zeros_like(block_state))
    incoming = prefix((decay_step, block_state), "gz", chain_combine, identity, False)
    state_low = incoming[1].astype(jnp.bfloat16)
    within = jnp.einsum(
        "chji,cihp->cjhp", mix_weights, heads_in, preferred_element_type=jnp.float32
    )
    carried = jnp.einsum("cjhn,chpn->cjhp", out_read, state_low, preferred_element_type=jnp.float32)
    ssd_out = (
        (within + carried + skip_gain[None, None, :, None] * heads_in)
        .reshape(columns, sections, channels)
        .astype(jnp.bfloat16)
    )
    margin = kernel.shape[0] // 2
    row_total = columns * sections * lax.axis_size("gz") * lax.axis_size("lat")
    plane_out = lax.all_to_all(ssd_out, "lat", split_axis=1, concat_axis=0, tiled=True)
    extent = plane_out.shape[0]
    widths = ((margin, margin), (0, 0), (0, 0))
    padded_out = jnp.pad(plane_out, widths)
    lateral_out = lateral_sum(padded_out, kernel, extent, False).astype(jnp.bfloat16)
    grad_planes = lateral_sum(jnp.pad(cotangent, widths), kernel, extent, True).astype(jnp.bfloat16)
    grad_ssd = lax.all_to_all(grad_planes, "lat", split_axis=0, concat_axis=1, tiled=True)
    kernel_part = kernel_terms(cotangent, padded_out, extent)
    grad_kernel = lax.psum(kernel_part, ("gz", "lat")) / math.sqrt(row_total)
    heads_grad = grad_ssd.reshape(columns, sections, head_count, head_size)
    block_adjoint = jnp.einsum(
        "cjhn,cjhp->chpn", out_read, heads_grad, preferred_element_type=jnp.float32
    )
    outgoing = prefix((decay_step, block_adjoint), "gz", chain_combine, identity, True)
    adjoint_low = outgoing[1].astype(jnp.bfloat16)
    grad_features = jnp.einsum(
        "chji,cjhp->cihp", mix_weights, heads_grad, preferred_element_type=jnp.float32
    )
    grad_features = grad_features + jnp.einsum(
        "cihn,chpn->cihp", in_weights, adjoint_low, preferred_element_type=jnp.float32
    )
    grad_features = (
        (grad_features + skip_gain[None, None, :, None] * heads_grad)
        .reshape(columns, sections, channels)
        .astype(jnp.bfloat16)
    )
    pair_weights = jax.vmap(head_pairs)(heads_grad, heads_in, log_decay, step_size)
    grad_read = (
        (heads_grad * jnp.exp(log_decay)[..., None])
        .astype(jnp.bfloat16)
        .reshape(columns, sections, channels)
    )
    feat_weights = (
        (heads_in * out_weight[..., None]).astype(jnp.bfloat16).reshape(columns, sections, channels)
    )
    state_rows = state_low.reshape(columns, channels, state_size)
    adjoint_rows = adjoint_low.reshape(columns, channels, state_size)
    grad_output_map = jnp.einsum(
        "cji,cin->cjn", pair_weights, input_map, preferred_element_type=jnp.float32
    )
    grad_output_map = (
        grad_output_map
        + jnp.einsum("cjk,ckn->cjn", grad_read, state_rows, preferred_element_type=jnp.float32)
    ).astype(jnp.bfloat16)
    grad_input_map = jnp.einsum(
        "cji,cjn->cin", pair_weights, output_map, preferred_element_type=jnp.float32
    )
    grad_input_map = (
        grad_input_map
        + jnp.einsum("cik,ckn->cin", feat_weights, adjoint_rows, preferred_element_type=jnp.float32)
    ).astype(jnp.bfloat16)
    return (lateral_out, grad_features, grad_input_map, grad_output_map, grad_kernel)


def solution(mesh):
    in_specs = (
        P("lat", "gz", None),
        P("lat", "gz", None),
        P("lat", "gz", None),
        P("lat", "gz", None),
        P(),
        P(),
        P(),
        P(None, ("gz", "lat"), None),
    )
    out_specs = (
        P(None, ("gz", "lat"), None),
        P("lat", "gz", None),
        P("lat", "gz", None),
        P("lat", "gz", None),
        P(),
    )
    return jax.shard_map(
        per_device, mesh=mesh, in_specs=in_specs, out_specs=out_specs, check_vma=False
    )
```

profile of v0, /device:TPU:0, one launch (start us, length us, event | category | flops | bytes accessed | tf_op | source)
XLA Modules:
  0.0 232.7 jit_solution(5359161026547841634)
XLA Ops:
  9.2 1.2 copy.101
  11.2 1.6 convolution_bitcast_fusion
  12.9 12.6 %all_gather.18 = f32[4,1,24]{2,1,0:T(1,128)S(1)} all-gather(f32[1,1,24]{2,1,0:T(1,128)S(1)} %get-tuple-element.337), channel_id=1, replica_groups=mesh['gz'=4,'lat'=8] {'gz'}, dimensions={0}, use_global_device_ids=true | all-gather | bytes 480 | tf_op jit(solution)/shard_map/all_gather | solution.py:13
  25.7 53.4 %all-gather.5.cloned.1.call-done = f32[96,64,128]{2,1,0:T(8,128)} async-done(((f32[24,64,128]{2,1,0:T(8,128)}), f32[96,64,128]{2,1,0:T(8,128)}) %all-gather.5.cloned.1.call-update) | async-done | bytes 3145744 | tf_op jit(solution)/shard_map/all_gather | solution.py:13
  82.1 3.0 %reduce.12 = bf16[128,1536]{1,0:T(8,128)(2,1)S(1)} reduce(bf16[128,1,1536]{2,1,0:T(2,128)(2,1)S(1)} %bitcast.167, bf16[]{:T(256)} %broadcast.126), dimensions={1}, to_apply=%bitcast.130.reduce_sub_computation | reduce | bytes 786434
  85.1 1.0 reshape.339
  86.1 3.7 %all-to-all-start = ((bf16[8,2,12288]{2,1,0:T(2,128)(2,1)}), bf16[8,2,12288]{2,1,0:T(2,128)(2,1)S(1)}, u32[]{:S(2)}, u32[]{:S(2)}) async-start(bf16[8,2,12288]{2,1,0:T(2,128)(2,1)} %reshape.339), calls=%async_computation | async-start | bytes 786432 | tf_op jit(solution)/shard_map/all_to_all | solution.py:122
  90.0 8.1 %all-to-all-done = bf16[8,2,12288]{2,1,0:T(2,128)(2,1)S(1)} async-done(((bf16[8,2,12288]{2,1,0:T(2,128)(2,1)}), bf16[8,2,12288]{2,1,0:T(2,128)(2,1)S(1)}, u32[]{:S(2)}, u32[]{:S(2)}) %all-to-all-start) | async-done | bytes 393248 | tf_op jit(solution)/shard_map/all_to_all | solution.py:122
  98.9 40.9 %psum.7 = f32[3,1536]{1,0:T(4,128)S(1)} all-reduce(f32[3,1536]{1,0:T(4,128)S(1)} %pad_maximum_fusion), channel_id=1, replica_groups=mesh['gz'=4,'lat'=8] {'gz','lat'}, use_global_device_ids=true, to_apply=%region_7.8 | all-reduce | flops 4608 | bytes 36864 | tf_op jit(solution)/shard_map/psum | solution.py:130
  139.7 1.2 add_convert_fusion
  140.9 3.6 %all-to-all-start.1 = ((bf16[8,16,1536]{2,1,0:T(8,128)(2,1)}), bf16[8,16,1536]{2,1,0:T(8,128)(2,1)S(1)}, u32[]{:S(2)}, u32[]{:S(2)}) async-start(bf16[8,16,1536]{2,1,0:T(8,128)(2,1)} %get-tuple-element.338), calls=%async_computation.1 | async-start | bytes 786432 | tf_op jit(solution)/shard_map/all_to_all | solution.py:128
  145.4 7.5 %all-to-all-done.1 = bf16[8,16,1536]{2,1,0:T(8,128)(2,1)S(1)} async-done(((bf16[8,16,1536]{2,1,0:T(8,128)(2,1)}), bf16[8,16,1536]{2,1,0:T(8,128)(2,1)S(1)}, u32[]{:S(2)}, u32[]{:S(2)}) %all-to-all-start.1) | async-done | bytes 393248 | tf_op jit(solution)/shard_map/all_to_all | solution.py:128
  153.3 1.1 copy.113
  155.3 1.6 fusion.20
  156.9 22.5 %while.39 = (s32[]{:T(128)}, f32[1,128,128]{2,1,0:T(8,128)S(1)}, bf16[24,1,128,64]{3,2,1,0:T(8,128)(2,1)}, bf16[24,1,128,64]{2,3,0,1:T(8,128)(2,1)S(1)}, f32[24,...) while((s32[]{:T(128)}, f32[1,128,128]{2,1,0:T(8,128)S(1)}, ...), condition=%wide.region_6.7_spmd.clone, body=%wide.region_5.6_spmd.clone.sunk | while | flops 2211843 | bytes 184931 | solution.py:61
  156.9 0.9 fusion.65
  157.9 0.9 fusion.65
  158.8 0.9 fusion.65
  159.7 0.9 fusion.65
  160.7 0.9 fusion.65
  161.6 0.9 fusion.65
  162.5 0.9 fusion.65
  163.5 0.9 fusion.65
  164.4 0.9 fusion.65
  165.4 0.9 fusion.65
  166.3 0.9 fusion.65
  167.2 0.9 fusion.65
  168.2 0.9 fusion.65
  169.1 0.9 fusion.65
  170.1 0.9 fusion.65
  171.0 0.9 fusion.65
  171.9 0.9 fusion.65
  172.9 0.9 fusion.65
  173.8 0.9 fusion.65
  174.7 0.9 fusion.65
  175.7 0.9 fusion.65
  176.6 0.9 fusion.65
  177.6 0.9 fusion.65
  178.5 0.9 fusion.65
  181.0 0.9 fusion.18
  182.1 1.6 fusion.34
  183.7 35.2 %all-gather.7.cloned.1.call-done = f32[96,64,128]{2,1,0:T(8,128)} async-done(((f32[24,64,128]{2,1,0:T(8,128)}), f32[96,64,128]{2,1,0:T(8,128)}) %all-gather.7.cloned.1.call-update) | async-done | bytes 3145744 | tf_op jit(solution)/shard_map/all_gather | solution.py:13
  219.0 4.2 %while.38 = (s32[]{:T(128)}, f32[1,24,64,128]{3,2,1,0:T(8,128)S(1)}, s32[]{:T(128)}, f32[4,1,24]{2,1,0:T(1,128)S(1)}, f32[4,1,24,64,128]{4,3,2,1,0:T(8,128)}, /*index=5*/s32[]{:T(128)}, s32[]{:T(128)}, s32[]{:T(128)}, s32[]{:T(128)}) while((s32[]{:T(128)}, f32[1,24,64,128]{3,2,1,0:T(8,128)S(1)}, s32[]{:T(128)}, f32[4,1,24]{2,1,0:T(1,128)S(1)}, ...), condition=%wide.region_4.5_spmd, body=%wide.region_3.4_spmd.sunk | while | flops 393222 | bytes 2359731 | solution.py:22
  219.0 1.4 bitcast_add_fusion.5
  220.4 1.3 bitcast_add_fusion.5
  221.8 1.3 bitcast_add_fusion.5
  224.0 0.9 copy.119
  224.9 0.9 fusion.19
  (94 shorter events, 12.0 us)
Async XLA Ops:
  7.2 71.9 %all-gather.5.cloned.1.call-start = ((), (), s32[]{:S(2)}) async-start(), calls=%async_computation.2 | async-start | bytes 3932160 | tf_op jit(solution)/shard_map/all_gather | solution.py:13
  9.2 16.4 %copy-start.3 = (bf16[1,128,128]{2,1,0:T(8,128)(2,1)S(1)}, bf16[1,128,128]{2,1,0:T(8,128)(2,1)}, u32[]{:S(2)}) copy-start(bf16[1,128,128]{2,1,0:T(8,128)(2,1)} %param.16) | copy-start | bytes 98308
  9.2 16.4 %copy-start.2 = (bf16[1,128,128]{2,1,0:T(8,128)(2,1)S(1)}, bf16[1,128,128]{2,1,0:T(8,128)(2,1)}, u32[]{:S(2)}) copy-start(bf16[1,128,128]{2,1,0:T(8,128)(2,1)} %param.15) | copy-start | bytes 98308
  25.7 54.3 %copy-start.4 = (f32[128,128]{1,0:T(8,128)}, f32[128,128]{1,0:T(8,128)S(1)}, u32[]{:S(2)}) copy-start(f32[128,128]{1,0:T(8,128)S(1)} %fusion.43) | copy-start | bytes 196612
  79.2 0.8 copy-start.6
  79.2 0.8 copy-start.8
  82.1 7.8 %copy-start.7 = (f32[3,1536]{1,0:T(4,128)S(1)}, f32[3,1536]{1,0:T(4,128)}, u32[]{:S(2)}) copy-start(f32[3,1536]{1,0:T(4,128)} %param.20) | copy-start | bytes 55300
  86.1 12.0 %all-to-all-start = ((bf16[8,2,12288]{2,1,0:T(2,128)(2,1)}), bf16[8,2,12288]{2,1,0:T(2,128)(2,1)S(1)}, u32[]{:S(2)}, u32[]{:S(2)}) async-start(bf16[8,2,12288]{2,1,0:T(2,128)(2,1)} %reshape.339), calls=%async_computation | async-start | bytes 786432 | tf_op jit(solution)/shard_map/all_to_all | solution.py:122
  89.7 8.8 %copy-start = (bf16[8,16,1536]{2,1,0:T(8,128)(2,1)S(1)}, bf16[8,16,1536]{2,1,0:T(8,128)(2,1)}, u32[]{:S(2)}) copy-start(bf16[8,16,1536]{2,1,0:T(8,128)(2,1)} %param.21) | copy-start | bytes 1179652
  140.9 11.9 %all-to-all-start.1 = ((bf16[8,16,1536]{2,1,0:T(8,128)(2,1)}), bf16[8,16,1536]{2,1,0:T(8,128)(2,1)S(1)}, u32[]{:S(2)}, u32[]{:S(2)}) async-start(bf16[8,16,1536]{2,1,0:T(8,128)(2,1)} %get-tuple-element.338), calls=%async_computation.1 | async-start | bytes 786432 | tf_op jit(solution)/shard_map/all_to_all | solution.py:128
  144.5 74.4 %all-gather.7.cloned.1.call-start = ((), (), s32[]{:S(2)}) async-start(), calls=%async_computation.3 | async-start | bytes 3932160 | tf_op jit(solution)/shard_map/all_gather | solution.py:13
  180.4 1.8 copy-start.5
  219.0 4.3 %copy-start.1 = (f32[24,64,128]{2,1,0:T(8,128)S(1)}, f32[24,64,128]{2,1,0:T(8,128)}, u32[]{:S(2)}) copy-start(f32[24,64,128]{2,1,0:T(8,128)} %fusion.34) | copy-start | bytes 2359300
  219.0 4.3 %copy-start.9 = (f32[24]{0:T(128)S(1)}, f32[24]{0:T(128)}, u32[]{:S(2)}) copy-start(f32[24]{0:T(128)} %param.19) | copy-start | bytes 292
Sparse Core Ops, SparseCore 0:
  12.9 66.1 all-gather.4
  157.0 61.8 all-gather.6
where the time goes:
time: 235 us; the launch traced here: 233 us
  waiting for transfers between devices  104 us (44%)
  blocking collectives  53.5 us (23%)
  matrix products  30.7 us (13%)
  between operations  14.4 us (6%)
  other arithmetic  11.6 us (5%)
  local copies, waits for them, and re-layouts  9.91 us (4%)
  starting transfers between devices  7.49 us (3%)
    all_gather x2, waiting for transfers between devices, prefix(): gathered = jax.tree.map(lambda a: lax.all_gather(a, axis), part)  88.5 us
    psum x1, blocking collectives, per_device(): grad_kernel = lax.psum(kernel_part, ('gz', 'lat')) / math.sqrt(row_total)  40.9 us
    dot_general x24, matrix products, accumulate(): jnp.dot(grad_head, feat_head.T, preferred_element_type=jnp.float32)  21.5 us
    all_gather x1, blocking collectives, prefix(): gathered = jax.tree.map(lambda a: lax.all_gather(a, axis), part)  12.6 us
    all_to_all x1, waiting for transfers between devices, per_device(): lax.all_to_all(ssd_out, 'lat', split_axis=1, concat_axis=0, tiled=True)  8.08 us
    all_to_all x1, waiting for transfers between devices, per_device(): lax.all_to_all(grad_planes, 'lat', split_axis=0, concat_axis=1, tiled=True)  7.47 us
    unnamed x29, local copies, waits for them, and re-layouts  6.1 us
  transfers between devices with their start and end apart: 4, of which 4 were waited for; matrix products, arithmetic and copies ran while one was open for 12% of the time, Pallas kernels for 0%

commit v1 on v0

v1 whole, which is shorter than its diff:
```python
import functools
import math

import jax
import jax.numpy as jnp
from jax import lax
from jax.experimental import pallas as pl
from jax.experimental.pallas import tpu as pltpu
from jax.sharding import PartitionSpec as P

F32 = jnp.float32
BF16 = jnp.bfloat16
MESH = pl.DeviceIdType.MESH
HOP_STEPS = 2
LATE_STEPS = 3


def dot(a, b, da, db):
    return lax.dot_general(a, b, (((da,), (db,)), ((), ())), preferred_element_type=F32)


def expand(values, onehot):
    high = values.astype(BF16)
    low = (values - high.astype(F32)).astype(BF16)
    return dot(high, onehot, 1, 0) + dot(low, onehot, 1, 0)


def kernel_body(
    gz_count, lat_count, width, row_total,
    feat_hbm, in_ref, out_ref, step_ref, rate_ref, skip_ref, ker_ref, cot_hbm,
    lat_ref, gf_ref, gim_ref, gom_ref, gk_ref,
    feat, cotp, gsend, grecv, osend, orecv, wide,
    fw, gr, grad, ec, wc, within, bs, ad, sin, sout, ain, aout, sp, ap, vecs, gk1, gk2,
    load_sem, gs_sem, gr_sem, os_sem, or_sem, fs_sem, fr_sem, bs_sem, br_sem, k_sem,
):
    gz = lax.axis_index("gz")
    me = lax.axis_index("lat")
    sections, channels = feat.shape
    heads = step_ref.shape[1]
    head_size = channels // heads
    rows = gsend.shape[1]
    taps = ker_ref.shape[0]
    chunks = channels // width
    aligned = rows % 16 == 0

    load_cot = pltpu.make_async_copy(cot_hbm, cotp.at[pl.ds(1, lat_count)], load_sem.at[0])
    load_feat = pltpu.make_async_copy(feat_hbm.at[0], feat, load_sem.at[1])
    load_cot.start()
    load_feat.start()

    barrier = pltpu.get_barrier_semaphore()

    def greet_lat(step, carry):
        pl.semaphore_signal(
            barrier, inc=1, device_id=(gz, lax.rem(me + step, lat_count)), device_id_type=MESH
        )
        return carry

    def greet_gz(step, carry):
        pl.semaphore_signal(
            barrier, inc=1, device_id=(lax.rem(gz + step, gz_count), me), device_id_type=MESH
        )
        return carry

    lax.fori_loop(1, lat_count, greet_lat, 0)
    lax.fori_loop(1, gz_count, greet_gz, 0)

    zero_plane = jnp.zeros((rows, channels), BF16)
    cotp[0] = zero_plane
    cotp[lat_count + 1] = zero_plane
    orecv[0] = zero_plane
    orecv[lat_count + 1] = zero_plane

    load_cot.wait()

    def grad_plane(x, carry):
        total = ker_ref[0:1, :] * cotp[x + 2].astype(F32)
        for tap in range(1, taps):
            total = total + ker_ref[tap : tap + 1, :] * cotp[x + 2 - tap].astype(F32)
        gsend[x] = total.astype(BF16)
        return carry

    lax.fori_loop(0, lat_count, grad_plane, 0, unroll=lat_count <= 8)
    pl.semaphore_wait(barrier, lat_count + gz_count - 2)

    def grad_copy(dest):
        return pltpu.make_async_remote_copy(
            src_ref=gsend.at[dest], dst_ref=grecv.at[me], send_sem=gs_sem, recv_sem=gr_sem,
            device_id=(gz, dest), device_id_type=MESH,
        )

    def grad_start(step, carry):
        grad_copy(lax.rem(me + step, lat_count)).start()
        return carry

    lax.fori_loop(1, lat_count, grad_start, 0)
    grecv[me] = gsend[me]

    row_index = lax.broadcasted_iota(jnp.int32, (sections, sections), 0)
    col_index = lax.broadcasted_iota(jnp.int32, (sections, sections), 1)
    lower = row_index >= col_index
    step_size = step_ref[...]
    log_decay = lax.dot_general(
        jnp.where(lower, 1.0, 0.0), -step_size * rate_ref[...], (((1,), (0,)), ((), ())),
        preferred_element_type=F32, precision=lax.Precision.HIGHEST,
    )
    middle = log_decay[sections // 2 - 1 : sections // 2]
    last = log_decay[sections - 1 : sections]
    head_index = lax.broadcasted_iota(jnp.int32, (heads, channels), 0)
    lane_index = lax.broadcasted_iota(jnp.int32, (heads, channels), 1)
    low_lane = head_index * head_size
    onehot = jnp.where(
        (lane_index >= low_lane) & (lane_index < low_lane + head_size), 1.0, 0.0
    ).astype(BF16)
    wc[...] = expand(step_size * jnp.exp(middle - log_decay), onehot)
    which = lax.broadcasted_iota(jnp.int32, (8, heads), 0)
    vectors = jnp.where(
        which == 0,
        jnp.exp(middle),
        jnp.where(which == 1, jnp.exp(last), jnp.where(which == 2, jnp.exp(last - middle), skip_ref[...])),
    )
    vecs[...] = expand(vectors, onehot)
    load_feat.wait()
    fw[...] = (wc[...] * feat[...].astype(F32)).astype(BF16)
    in_map = in_ref[...]
    out_map = out_ref[...]
    in_turned = in_map.astype(F32).T.astype(BF16)
    out_turned = out_map.astype(F32).T.astype(BF16)
    bs[...] = dot(in_turned, fw[...], 1, 0) * vecs[2:3, :]
    product = jnp.where(lower, dot(out_map, in_map, 1, 1), 0.0)
    mix = product.astype(BF16)
    mix_turned = product.T.astype(BF16)

    def forward_copy(c):
        return pltpu.make_async_remote_copy(
            src_ref=sout.at[c], dst_ref=sin.at[c], send_sem=fs_sem.at[c], recv_sem=fr_sem.at[c],
            device_id=(lax.rem(gz + 1, gz_count), me), device_id_type=MESH,
        )

    def backward_copy(c):
        return pltpu.make_async_remote_copy(
            src_ref=aout.at[c], dst_ref=ain.at[c], send_sem=bs_sem.at[c], recv_sem=br_sem.at[c],
            device_id=(lax.rem(gz + gz_count - 1, gz_count), me), device_id_type=MESH,
        )

    def out_copy(c, lanes, dest):
        return pltpu.make_async_remote_copy(
            src_ref=osend.at[dest, :, lanes], dst_ref=orecv.at[me + 1, :, lanes],
            send_sem=os_sem.at[c], recv_sem=or_sem.at[c],
            device_id=(gz, dest), device_id_type=MESH,
        )

    def span(c):
        return pl.ds(pl.multiple_of(c * width, width), width)

    def first_use():
        ec[...] = expand(jnp.exp(log_decay - middle), onehot)
        within[...] = dot(mix, fw[...], 1, 0)

    def gradients():
        pltpu.make_async_remote_copy(
            src_ref=gsend.at[pl.ds(0, lat_count - 1)], dst_ref=grecv.at[pl.ds(0, lat_count - 1)],
            send_sem=gs_sem, recv_sem=gr_sem, device_id=(gz, me), device_id_type=MESH,
        ).wait_recv()
        if aligned:
            grad[...] = grecv[...].reshape(sections, channels).astype(F32)
        else:
            for source in range(lat_count):
                grad[source * rows : (source + 1) * rows, :] = grecv[source].astype(F32)
        gr[...] = (ec[...] * grad[...]).astype(BF16)
        ad[...] = dot(out_turned, gr[...], 1, 0) * vecs[0:1, :]

    def forward_chunk(c):
        lanes = span(c)

        @pl.when(gz > 0)
        def _():
            forward_copy(c).wait_recv()

        @pl.when(gz == 0)
        def _():
            sin[c] = jnp.zeros((sin.shape[1], width), BF16)

        state = sin[c].astype(F32)

        @pl.when(gz < gz_count - 1)
        def _():
            sout[c] = (state * vecs[1:2, lanes] + bs[:, lanes]).astype(BF16)
            forward_copy(c).start()

        low = (state * vecs[0:1, lanes]).astype(BF16)
        sp[:, lanes] = low
        total = ec[:, lanes] * (within[:, lanes] + dot(out_map, low, 1, 0))
        total = total + vecs[3:4, lanes] * feat[:, lanes].astype(F32)
        if aligned:
            osend[:, :, lanes] = total.astype(BF16).reshape(lat_count, rows, width)
        else:
            wide[...] = total
            for dest in range(lat_count):
                osend[dest, :, lanes] = wide[dest * rows : (dest + 1) * rows, :].astype(BF16)

        def start(step, carry):
            out_copy(c, lanes, lax.rem(me + step, lat_count)).start()
            return carry

        lax.fori_loop(1, lat_count, start, 0)
        orecv[me + 1, :, lanes] = osend[me, :, lanes]

    def backward_chunk(c):
        lanes = span(c)

        @pl.when(gz < gz_count - 1)
        def _():
            backward_copy(c).wait_recv()

        @pl.when(gz == gz_count - 1)
        def _():
            ain[c] = jnp.zeros((ain.shape[1], width), BF16)

        state = ain[c].astype(F32)

        @pl.when(gz > 0)
        def _():
            aout[c] = (state * vecs[1:2, lanes] + ad[:, lanes]).astype(BF16)
            backward_copy(c).start()

        ap[:, lanes] = (state * vecs[2:3, lanes]).astype(BF16)

    first_use()

    def tick(step, carry):
        c = step - gz * HOP_STEPS

        @pl.when((c >= 0) & (c < chunks))
        def _():
            forward_chunk(c)

        @pl.when(step == LATE_STEPS)
        def _():
            gradients()

        e = step - LATE_STEPS - (gz_count - 1 - gz) * HOP_STEPS

        @pl.when((e >= 0) & (e < chunks))
        def _():
            backward_chunk(e)

        return carry

    lax.fori_loop(0, chunks + LATE_STEPS + (gz_count - 1) * HOP_STEPS, tick, 0)

    def plane_chunk(c, carry):
        lanes = span(c)
        pltpu.make_async_remote_copy(
            src_ref=osend.at[pl.ds(0, lat_count - 1), :, lanes],
            dst_ref=orecv.at[pl.ds(1, lat_count - 1), :, lanes],
            send_sem=os_sem.at[c], recv_sem=or_sem.at[c], device_id=(gz, me), device_id_type=MESH,
        ).wait_recv()

        def plane(x, sums):
            cot = cotp[x + 1, :, lanes].astype(F32)
            total = 0.0
            new = []
            for tap in range(taps):
                piece = orecv[x + tap, :, lanes].astype(F32)
                total = total + ker_ref[tap : tap + 1, lanes] * piece
                new.append(sums[tap] + cot * piece)
            lat_ref[x, :, lanes] = total.astype(BF16)
            return tuple(new)

        sums = lax.fori_loop(
            0, lat_count, plane, tuple(jnp.zeros((rows, width), F32) for _ in range(taps)),
            unroll=lat_count <= 8,
        )
        for tap in range(taps):
            gk1[me, tap : tap + 1, lanes] = jnp.sum(sums[tap], axis=0, keepdims=True)
        return carry

    lax.fori_loop(0, chunks, plane_chunk, 0)

    def lat_start(step, carry):
        pltpu.make_async_remote_copy(
            src_ref=gk1.at[me], dst_ref=gk1.at[me], send_sem=k_sem.at[0], recv_sem=k_sem.at[1],
            device_id=(gz, lax.rem(me + step, lat_count)), device_id_type=MESH,
        ).start()
        return carry

    lax.fori_loop(1, lat_count, lat_start, 0)

    pair = jnp.where(lower, dot(gr[...], fw[...], 1, 1), 0.0)
    gom = dot(pair.astype(BF16), in_map, 1, 0) + dot(gr[...], sp[...], 1, 1)
    gom_ref[...] = gom.astype(BF16)

    lat_all = pltpu.make_async_remote_copy(
        src_ref=gk1.at[pl.ds(0, lat_count - 1)], dst_ref=gk1.at[pl.ds(0, lat_count - 1)],
        send_sem=k_sem.at[0], recv_sem=k_sem.at[1], device_id=(gz, me), device_id_type=MESH,
    )
    lat_all.wait_recv()
    gk2[gz] = jnp.sum(gk1[...], axis=0)

    def gz_start(step, carry):
        pltpu.make_async_remote_copy(
            src_ref=gk2.at[gz], dst_ref=gk2.at[gz], send_sem=k_sem.at[2], recv_sem=k_sem.at[3],
            device_id=(lax.rem(gz + step, gz_count), me), device_id_type=MESH,
        ).start()
        return carry

    lax.fori_loop(1, gz_count, gz_start, 0)

    gim = dot(pair.T.astype(BF16), out_map, 1, 0) + dot(fw[...], ap[...], 1, 1)
    gim_ref[...] = gim.astype(BF16)
    gf = dot(mix_turned, gr[...], 1, 0) + dot(in_map, ap[...], 1, 0)
    gf_ref[...] = (wc[...] * gf + vecs[3:4, :] * grad[...]).astype(BF16)

    gz_all = pltpu.make_async_remote_copy(
        src_ref=gk2.at[pl.ds(0, gz_count - 1)], dst_ref=gk2.at[pl.ds(0, gz_count - 1)],
        send_sem=k_sem.at[2], recv_sem=k_sem.at[3], device_id=(gz, me), device_id_type=MESH,
    )
    gz_all.wait_recv()
    gk_ref[...] = jnp.sum(gk2[...], axis=0) * (1.0 / math.sqrt(row_total))

    lat_all.wait_send()
    gz_all.wait_send()
    pltpu.make_async_remote_copy(
        src_ref=gsend.at[pl.ds(0, lat_count - 1)], dst_ref=grecv.at[pl.ds(0, lat_count - 1)],
        send_sem=gs_sem, recv_sem=gr_sem, device_id=(gz, me), device_id_type=MESH,
    ).wait_send()

    def drain(c, carry):
        lanes = span(c)
        pltpu.make_async_remote_copy(
            src_ref=osend.at[pl.ds(0, lat_count - 1), :, lanes],
            dst_ref=orecv.at[pl.ds(1, lat_count - 1), :, lanes],
            send_sem=os_sem.at[c], recv_sem=or_sem.at[c], device_id=(gz, me), device_id_type=MESH,
        ).wait_send()

        @pl.when(gz < gz_count - 1)
        def _():
            forward_copy(c).wait_send()

        @pl.when(gz > 0)
        def _():
            backward_copy(c).wait_send()

        return carry

    lax.fori_loop(0, chunks, drain, 0)


def per_device(
    features, input_map, output_map, step_size, decay_rate, skip_gain, kernel, cotangent
):
    columns, sections, channels = features.shape
    assert columns == 1
    heads = step_size.shape[2]
    states = input_map.shape[2]
    taps = kernel.shape[0]
    assert taps == 3
    gz_count = lax.axis_size("gz")
    lat_count = lax.axis_size("lat")
    extent, rows, _ = cotangent.shape
    assert extent == lat_count
    width = 256
    chunks = channels // width
    row_total = columns * sections * gz_count * lat_count
    vmem = pl.BlockSpec(memory_space=pltpu.VMEM)
    hbm = pl.BlockSpec(memory_space=pl.ANY)
    full = (sections, channels)
    turned = (states, channels)
    lateral_out, grad_features, grad_in, grad_out, grad_kernel = pl.pallas_call(
        functools.partial(kernel_body, gz_count, lat_count, width, row_total),
        out_shape=(
            jax.ShapeDtypeStruct(cotangent.shape, BF16),
            jax.ShapeDtypeStruct(full, BF16),
            jax.ShapeDtypeStruct((sections, states), BF16),
            jax.ShapeDtypeStruct((sections, states), BF16),
            jax.ShapeDtypeStruct((taps, channels), F32),
        ),
        in_specs=[hbm, vmem, vmem, vmem, vmem, vmem, vmem, hbm],
        out_specs=(vmem,) * 5,
        scratch_shapes=[
            pltpu.VMEM(full, BF16),
            pltpu.VMEM((extent + 2, rows, channels), BF16),
            pltpu.VMEM((lat_count, rows, channels), BF16),
            pltpu.VMEM((lat_count, rows, channels), BF16),
            pltpu.VMEM((lat_count, rows, channels), BF16),
            pltpu.VMEM((extent + 2, rows, channels), BF16),
            pltpu.VMEM((sections, width), F32),
            pltpu.VMEM(full, BF16),
            pltpu.VMEM(full, BF16),
            pltpu.VMEM(full, F32),
            pltpu.VMEM(full, F32),
            pltpu.VMEM(full, F32),
            pltpu.VMEM(full, F32),
            pltpu.VMEM(turned, F32),
            pltpu.VMEM(turned, F32),
            pltpu.VMEM((chunks, states, width), BF16),
            pltpu.VMEM((chunks, states, width), BF16),
            pltpu.VMEM((chunks, states, width), BF16),
            pltpu.VMEM((chunks, states, width), BF16),
            pltpu.VMEM(turned, BF16),
            pltpu.VMEM(turned, BF16),
            pltpu.VMEM((8, channels), F32),
            pltpu.VMEM((lat_count, taps, channels), F32),
            pltpu.VMEM((gz_count, taps, channels), F32),
            pltpu.SemaphoreType.DMA((2,)),
            pltpu.SemaphoreType.DMA,
            pltpu.SemaphoreType.DMA,
            pltpu.SemaphoreType.DMA((chunks,)),
            pltpu.SemaphoreType.DMA((chunks,)),
            pltpu.SemaphoreType.DMA((chunks,)),
            pltpu.SemaphoreType.DMA((chunks,)),
            pltpu.SemaphoreType.DMA((chunks,)),
            pltpu.SemaphoreType.DMA((chunks,)),
            pltpu.SemaphoreType.DMA((4,)),
        ],
        compiler_params=pltpu.CompilerParams(collective_id=0, has_side_effects=True),
    )(
        features,
        input_map.reshape(sections, states),
        output_map.reshape(sections, states),
        step_size.reshape(sections, heads),
        decay_rate.reshape(1, heads),
        skip_gain.reshape(1, heads),
        kernel,
        cotangent,
    )
    return (
        lateral_out,
        grad_features.reshape(features.shape),
        grad_in.reshape(input_map.shape),
        grad_out.reshape(output_map.shape),
        grad_kernel,
    )


def solution(mesh):
    in_specs = (
        P("lat", "gz", None),
        P("lat", "gz", None),
        P("lat", "gz", None),
        P("lat", "gz", None),
        P(),
        P(),
        P(),
        P(None, ("gz", "lat"), None),
    )
    out_specs = (
        P(None, ("gz", "lat"), None),
        P("lat", "gz", None),
        P("lat", "gz", None),
        P("lat", "gz", None),
        P(),
    )
    return jax.shard_map(
        per_device, mesh=mesh, in_specs=in_specs, out_specs=out_specs, check_vma=False
    )
```

time: 235 us -> 46.3 us (0.20)
  waiting for transfers between devices: 104 us -> 0 us
  blocking collectives: 53.5 us -> 0 us
  Pallas kernels: 0 us -> 39.1 us
  matrix products: 30.7 us -> 0 us
  between operations: 14.4 us -> 0.65 us
  other arithmetic: 11.6 us -> 0 us
  starting transfers between devices: 7.49 us -> 0 us
  local copies, waits for them, and re-layouts: 9.91 us -> 6.14 us
    all_gather x2 -> x0, waiting for transfers between devices: 88.5 us -> none  [prefix(): gathered = jax.tree.map(lambda a: lax.all_gather(a, axis), part)]
    psum x1 -> x0, blocking collectives: 40.9 us -> none  [per_device(): grad_kernel = lax.psum(kernel_part, ('gz', 'lat')) / math.sqrt(row_total)]
    pallas_call x0 -> x1, Pallas kernels: none -> 39.1 us  [per_device(): pl.pallas_call(functools.partial(kernel_body, gz_count, lat_count, width,...]
    dot_general x35 -> x0, matrix products: 30.7 us -> none  [the longest x24 21.5 us: accumulate(): jnp.dot(grad_head, feat_head.T, preferred_element_type=jnp.float32)]
    all_to_all x2 -> x0, waiting for transfers between devices: 15.5 us -> none  [the longest x1 8.08 us: per_device(): lax.all_to_all(ssd_out, 'lat', split_axis=1, concat_axis=0, tiled=True)]
    all_gather x1 -> x0, blocking collectives: 12.6 us -> none  [prefix(): gathered = jax.tree.map(lambda a: lax.all_gather(a, axis), part)]
    all_to_all x2 -> x0, starting transfers between devices: 7.24 us -> none  [the longest x1 3.65 us: per_device(): lax.all_to_all(ssd_out, 'lat', split_axis=1, concat_axis=0, tiled=True)]
    add x3 -> x0, other arithmetic: 4.01 us -> none  [chain_combine(): later[0][:, :, None, None] * earlier[1] + later[1]]
  transfers between devices with their start and end apart: 4 -> 0, of which waited for: 4 -> 0; matrix products, arithmetic and copies ran while one was open for 12% -> 0% of each run, Pallas kernels for 0% -> 0%
where the time goes in v1:
time: 46.3 us; the launch traced here: 45.9 us
  Pallas kernels  39.1 us (84%)
  local copies, waits for them, and re-layouts  6.14 us (13%)
  between operations  0.65 us (1%)
    pallas_call x1, Pallas kernels, per_device(): pl.pallas_call(functools.partial(kernel_body, gz_count, lat_count, width,...  39.1 us
    unnamed x14, local copies, waits for them, and re-layouts  6.14 us

profile of v1, /device:TPU:0, one launch (start us, length us, event | category | flops | bytes accessed | tf_op | source)
XLA Modules:
  0.0 45.9 jit_solution(17716190694940358798)
XLA Ops:
  0.6 1.4 %copy.13 = f32[1,128,24]{2,1,0:T(8,128)} copy(f32[1,128,24]{1,2,0:T(8,128)} %param.11) | data formatting | bytes 24576 | tf_op args[3]
  2.1 39.1 %shard_map.119 = (bf16[8,16,1536]{2,1,0:T(8,128)(2,1)}, bf16[128,1536]{1,0:T(8,128)(2,1)}, bf16[128,128]{1,0:T(8,128)(2,1)}, bf16[128,128]{1,0:T(8,128)(2,1)}, f32[3,1536]{1,0:T(4,128)}) custom-call(bf16[1,128,1536]{2,1,0:T(8,128)(2,1)} %feat_hbm.1, bf16[128,128]{1,0:T(8,128)(2,1)} %bitcast.10, bf16[128,128]{1,0:T(8,128)(2,1)} %bitcast.11, ...), custom_call_target="tpu_custom_call" | custom-call | tf_op jit(solution)/shard_map/pallas_call | solution.py:370
  41.1 0.0 copy-start
  41.2 1.8 %copy.19 = bf16[8,16,1536]{2,1,0:T(8,128)(2,1)} copy(bf16[8,16,1536]{2,1,0:T(8,128)(2,1)} %get-tuple-element.20) | data formatting | bytes 786432
  43.0 0.0 copy-done
  43.0 0.0 copy-start.2
  43.0 0.7 %copy.20 = bf16[1,128,1536]{2,1,0:T(8,128)(2,1)} copy(bf16[1,128,1536]{2,1,0:T(8,128)(2,1)S(1)} %bitcast.8) | data formatting | bytes 786432
  43.7 0.0 copy-done.2
  43.7 0.0 copy-start.1
  43.7 0.6 %copy.21 = bf16[1,128,128]{2,1,0:T(8,128)(2,1)} copy(bf16[1,128,128]{2,1,0:T(8,128)(2,1)S(1)} %bitcast.13) | data formatting | bytes 65536
  44.4 0.2 copy-done.1
  44.5 0.0 copy-start.3
  44.5 0.6 %copy.22 = bf16[1,128,128]{2,1,0:T(8,128)(2,1)} copy(bf16[1,128,128]{2,1,0:T(8,128)(2,1)S(1)} %bitcast.12) | data formatting | bytes 65536
  45.1 0.1 copy-done.3
  45.3 0.6 %copy.23 = f32[3,1536]{1,0:T(4,128)} copy(f32[3,1536]{1,0:T(4,128)S(1)} %copy-done.3) | data formatting | bytes 36864
Async XLA Ops:
  41.1 1.8 %copy-start = (bf16[128,1536]{1,0:T(8,128)(2,1)S(1)}, bf16[128,1536]{1,0:T(8,128)(2,1)}, u32[]{:S(2)}) copy-start(bf16[128,1536]{1,0:T(8,128)(2,1)} %get-tuple-element.11) | copy-start | bytes 1179652
  43.0 0.8 %copy-start.2 = (bf16[128,128]{1,0:T(8,128)(2,1)S(1)}, bf16[128,128]{1,0:T(8,128)(2,1)}, u32[]{:S(2)}) copy-start(bf16[128,128]{1,0:T(8,128)(2,1)} %get-tuple-element.12) | copy-start | bytes 98308
  43.7 0.8 %copy-start.1 = (bf16[128,128]{1,0:T(8,128)(2,1)S(1)}, bf16[128,128]{1,0:T(8,128)(2,1)}, u32[]{:S(2)}) copy-start(bf16[128,128]{1,0:T(8,128)(2,1)} %get-tuple-element.13) | copy-start | bytes 98308
  44.5 0.8 %copy-start.3 = (f32[3,1536]{1,0:T(4,128)S(1)}, f32[3,1536]{1,0:T(4,128)}, u32[]{:S(2)}) copy-start(f32[3,1536]{1,0:T(4,128)} %get-tuple-element.24) | copy-start | bytes 55300

commit v2 on v1

--- a/solution.py
+++ b/solution.py
@@ -36,7 +36,7 @@
     gz = lax.axis_index("gz")
     me = lax.axis_index("lat")
     sections, channels = feat.shape
-    heads = step_ref.shape[1]
+    heads = step_ref.shape[0]
     head_size = channels // heads
     rows = gsend.shape[1]
     taps = ker_ref.shape[0]
@@ -99,7 +99,7 @@
     row_index = lax.broadcasted_iota(jnp.int32, (sections, sections), 0)
     col_index = lax.broadcasted_iota(jnp.int32, (sections, sections), 1)
     lower = row_index >= col_index
-    step_size = step_ref[...]
+    step_size = step_ref[...].T
     log_decay = lax.dot_general(
         jnp.where(lower, 1.0, 0.0), -step_size * rate_ref[...], (((1,), (0,)), ((), ())),
         preferred_element_type=F32, precision=lax.Precision.HIGHEST,
@@ -345,6 +345,18 @@
         return carry
 
     lax.fori_loop(0, chunks, drain, 0)
+
+
+def write_out(*refs):
+    sources, results, sem = refs[:5], refs[5:10], refs[10]
+    copies = [
+        pltpu.make_async_copy(source, result, sem.at[place])
+        for place, (source, result) in enumerate(zip(sources, results))
+    ]
+    for copy in copies:
+        copy.start()
+    for copy in copies:
+        copy.wait()
 
 
 def per_device(
@@ -367,14 +379,14 @@
     hbm = pl.BlockSpec(memory_space=pl.ANY)
     full = (sections, channels)
     turned = (states, channels)
-    lateral_out, grad_features, grad_in, grad_out, grad_kernel = pl.pallas_call(
+    held = pl.pallas_call(
         functools.partial(kernel_body, gz_count, lat_count, width, row_total),
         out_shape=(
-            jax.ShapeDtypeStruct(cotangent.shape, BF16),
-            jax.ShapeDtypeStruct(full, BF16),
-            jax.ShapeDtypeStruct((sections, states), BF16),
-            jax.ShapeDtypeStruct((sections, states), BF16),
-            jax.ShapeDtypeStruct((taps, channels), F32),
+            pltpu.VMEM(cotangent.shape, BF16),
+            pltpu.VMEM(full, BF16),
+            pltpu.VMEM((sections, states), BF16),
+            pltpu.VMEM((sections, states), BF16),
+            pltpu.VMEM((taps, channels), F32),
         ),
         in_specs=[hbm, vmem, vmem, vmem, vmem, vmem, vmem, hbm],
         out_specs=(vmem,) * 5,
@@ -419,12 +431,25 @@
         features,
         input_map.reshape(sections, states),
         output_map.reshape(sections, states),
-        step_size.reshape(sections, heads),
+        jnp.swapaxes(step_size, 1, 2).reshape(heads, sections),
         decay_rate.reshape(1, heads),
         skip_gain.reshape(1, heads),
         kernel,
         cotangent,
     )
+    lateral_out, grad_features, grad_in, grad_out, grad_kernel = pl.pallas_call(
+        write_out,
+        out_shape=(
+            jax.ShapeDtypeStruct(cotangent.shape, BF16),
+            jax.ShapeDtypeStruct(full, BF16),
+            jax.ShapeDtypeStruct((sections, states), BF16),
+            jax.ShapeDtypeStruct((sections, states), BF16),
+            jax.ShapeDtypeStruct((taps, channels), F32),
+        ),
+        in_specs=[vmem] * 5,
+        out_specs=(hbm,) * 5,
+        scratch_shapes=[pltpu.SemaphoreType.DMA((5,))],
+    )(*(pltpu.with_memory_space_constraint(one, pltpu.VMEM) for one in held))
     return (
         lateral_out,
         grad_features.reshape(features.shape),

time: 46.3 us -> 39.9 us (0.86)
  local copies, waits for them, and re-layouts: 6.14 us -> 0 us
    unnamed x14 -> x0, local copies, waits for them, and re-layouts: 6.14 us -> none
    pallas_call x1, Pallas kernels: 39.1 us -> 38.1 us  [per_device(): pl.pallas_call(functools.partial(kernel_body, gz_count, lat_count, width,...]
    pallas_call x0 -> x1, Pallas kernels: none -> 0.94 us  [per_device(): pl.pallas_call(write_out, out_shape=(jax.ShapeDtypeStruct(cotangent.shape...]
where the time goes in v2:
time: 39.9 us; the launch traced here: 39.6 us
  Pallas kernels  39 us (98%)
  between operations  0.64 us (2%)
    pallas_call x1, Pallas kernels, per_device(): pl.pallas_call(functools.partial(kernel_body, gz_count, lat_count, width,...  38.1 us
    pallas_call x1, Pallas kernels, per_device(): pl.pallas_call(write_out, out_shape=(jax.ShapeDtypeStruct(cotangent.shape...  0.94 us

profile of v2, /device:TPU:0, one launch (start us, length us, event | category | flops | bytes accessed | tf_op | source)
XLA Modules:
  0.0 39.6 jit_solution(1800602505906161425)
XLA Ops:
  0.6 38.1 %shard_map.119 = (bf16[8,16,1536]{2,1,0:T(8,128)(2,1)S(1)}, bf16[128,1536]{1,0:T(8,128)(2,1)S(1)}, bf16[128,128]{1,0:T(8,128)(2,1)S(1)}, bf16[128,128]{1,0:T(8,128)(2,1)S(1)}, f32[3,1536]{1,0:T(4,128)S(1)}) custom-call(bf16[1,128,1536]{2,1,0:T(8,128)(2,1)} %feat_hbm.1, bf16[128,128]{1,0:T(8,128)(2,1)} %bitcast.10, bf16[128,128]{1,0:T(8,128)(2,1)} %bitcast.11, ...), custom_call_target="tpu_custom_call" | custom-call | tf_op jit(solution)/shard_map/pallas_call | solution.py:382
  38.7 0.9 %shard_map.120 = (bf16[8,16,1536]{2,1,0:T(8,128)(2,1)}, bf16[128,1536]{1,0:T(8,128)(2,1)}, bf16[128,128]{1,0:T(8,128)(2,1)}, bf16[128,128]{1,0:T(8,128)(2,1)}, f32[3,1536]{1,0:T(4,128)}) custom-call(bf16[8,16,1536]{2,1,0:T(8,128)(2,1)S(1)} %get-tuple-element.15.refs_0_, bf16[128,1536]{1,0:T(8,128)(2,1)S(1)} %get-tuple-element.16.refs_1_, ...), custom_call_target="tpu_custom_call" | custom-call | tf_op jit(solution)/shard_map/pallas_call | solution.py:440

commit v3 on v2

--- a/solution.py
+++ b/solution.py
@@ -12,7 +12,9 @@
 BF16 = jnp.bfloat16
 MESH = pl.DeviceIdType.MESH
 HOP_STEPS = 2
-LATE_STEPS = 3
+LATE_STEPS = 4
+PLANE_STEPS = 3
+SUM_STEPS = 2
 
 
 def dot(a, b, da, db):
@@ -27,10 +29,11 @@
 
 def kernel_body(
     gz_count, lat_count, width, row_total,
-    feat_hbm, in_ref, out_ref, step_ref, rate_ref, skip_ref, ker_ref, cot_hbm,
+    feat_hbm, in_hbm, out_hbm, step_hbm, rate_hbm, skip_hbm, ker_hbm, cot_hbm,
     lat_ref, gf_ref, gim_ref, gom_ref, gk_ref,
     feat, cotp, gsend, grecv, osend, orecv, wide,
-    fw, gr, grad, ec, wc, within, bs, ad, sin, sout, ain, aout, sp, ap, vecs, gk1, gk2,
+    fw, gr, grad, ec, wc, within, bs, ad, sin, sout, ain, aout, sp, ap, vecs, gk1, gk2, pair_turned,
+    in_ref, out_ref, step_ref, rate_ref, skip_ref, ker_ref,
     load_sem, gs_sem, gr_sem, os_sem, or_sem, fs_sem, fr_sem, bs_sem, br_sem, k_sem,
 ):
     gz = lax.axis_index("gz")
@@ -45,8 +48,25 @@
 
     load_cot = pltpu.make_async_copy(cot_hbm, cotp.at[pl.ds(1, lat_count)], load_sem.at[0])
     load_feat = pltpu.make_async_copy(feat_hbm.at[0], feat, load_sem.at[1])
+    small = [
+        pltpu.make_async_copy(source, target, load_sem.at[2 + place])
+        for place, (source, target) in enumerate(
+            (
+                (step_hbm, step_ref),
+                (rate_hbm, rate_ref),
+                (skip_hbm, skip_ref),
+                (ker_hbm, ker_ref),
+                (in_hbm, in_ref),
+                (out_hbm, out_ref),
+            )
+        )
+    ]
+    for copy in small[:4]:
+        copy.start()
     load_cot.start()
+    small[4].start()
     load_feat.start()
+    small[5].start()
 
     barrier = pltpu.get_barrier_semaphore()
 
@@ -71,31 +91,8 @@
     orecv[0] = zero_plane
     orecv[lat_count + 1] = zero_plane
 
-    load_cot.wait()
-
-    def grad_plane(x, carry):
-        total = ker_ref[0:1, :] * cotp[x + 2].astype(F32)
-        for tap in range(1, taps):
-            total = total + ker_ref[tap : tap + 1, :] * cotp[x + 2 - tap].astype(F32)
-        gsend[x] = total.astype(BF16)
-        return carry
-
-    lax.fori_loop(0, lat_count, grad_plane, 0, unroll=lat_count <= 8)
-    pl.semaphore_wait(barrier, lat_count + gz_count - 2)
-
-    def grad_copy(dest):
-        return pltpu.make_async_remote_copy(
-            src_ref=gsend.at[dest], dst_ref=grecv.at[me], send_sem=gs_sem, recv_sem=gr_sem,
-            device_id=(gz, dest), device_id_type=MESH,
-        )
-
-    def grad_start(step, carry):
-        grad_copy(lax.rem(me + step, lat_count)).start()
-        return carry
-
-    lax.fori_loop(1, lat_count, grad_start, 0)
-    grecv[me] = gsend[me]
-
+    for copy in small[:4]:
+        copy.wait()
     row_index = lax.broadcasted_iota(jnp.int32, (sections, sections), 0)
     col_index = lax.broadcasted_iota(jnp.int32, (sections, sections), 1)
     lower = row_index >= col_index
@@ -120,16 +117,42 @@
         jnp.where(which == 1, jnp.exp(last), jnp.where(which == 2, jnp.exp(last - middle), skip_ref[...])),
     )
     vecs[...] = expand(vectors, onehot)
+    ec[...] = expand(jnp.exp(log_decay - middle), onehot)
+
+    load_cot.wait()
+
+    def grad_plane(x, carry):
+        total = ker_ref[0:1, :] * cotp[x + 2].astype(F32)
+        for tap in range(1, taps):
+            total = total + ker_ref[tap : tap + 1, :] * cotp[x + 2 - tap].astype(F32)
+        gsend[x] = total.astype(BF16)
+        return carry
+
+    lax.fori_loop(0, lat_count, grad_plane, 0, unroll=lat_count <= 8)
+    pl.semaphore_wait(barrier, lat_count + gz_count - 2)
+
+    def grad_copy(dest):
+        return pltpu.make_async_remote_copy(
+            src_ref=gsend.at[dest], dst_ref=grecv.at[me], send_sem=gs_sem, recv_sem=gr_sem,
+            device_id=(gz, dest), device_id_type=MESH,
+        )
+
+    def grad_start(step, carry):
+        grad_copy(lax.rem(me + step, lat_count)).start()
+        return carry
+
+    lax.fori_loop(1, lat_count, grad_start, 0)
+    grecv[me] = gsend[me]
+
     load_feat.wait()
+    small[4].wait()
+    small[5].wait()
     fw[...] = (wc[...] * feat[...].astype(F32)).astype(BF16)
     in_map = in_ref[...]
     out_map = out_ref[...]
     in_turned = in_map.astype(F32).T.astype(BF16)
     out_turned = out_map.astype(F32).T.astype(BF16)
     bs[...] = dot(in_turned, fw[...], 1, 0) * vecs[2:3, :]
-    product = jnp.where(lower, dot(out_map, in_map, 1, 1), 0.0)
-    mix = product.astype(BF16)
-    mix_turned = product.T.astype(BF16)
 
     def forward_copy(c):
         return pltpu.make_async_remote_copy(
@@ -152,10 +175,6 @@
 
     def span(c):
         return pl.ds(pl.multiple_of(c * width, width), width)
-
-    def first_use():
-        ec[...] = expand(jnp.exp(log_decay - middle), onehot)
-        within[...] = dot(mix, fw[...], 1, 0)
 
     def gradients():
         pltpu.make_async_remote_copy(
@@ -170,6 +189,15 @@
         gr[...] = (ec[...] * grad[...]).astype(BF16)
         ad[...] = dot(out_turned, gr[...], 1, 0) * vecs[0:1, :]
 
+        @pl.when(gz == gz_count - 1)
+        def _():
+            def send(c, carry):
+                aout[c] = ad[:, span(c)].astype(BF16)
+                backward_copy(c).start()
+                return carry
+
+            lax.fori_loop(0, chunks, send, 0)
+
     def forward_chunk(c):
         lanes = span(c)
 
@@ -183,7 +211,7 @@
 
         state = sin[c].astype(F32)
 
-        @pl.when(gz < gz_count - 1)
+        @pl.when((gz > 0) & (gz < gz_count - 1))
         def _():
             sout[c] = (state * vecs[1:2, lanes] + bs[:, lanes]).astype(BF16)
             forward_copy(c).start()
@@ -219,37 +247,28 @@
 
         state = ain[c].astype(F32)
 
-        @pl.when(gz > 0)
+        @pl.when((gz > 0) & (gz < gz_count - 1))
         def _():
             aout[c] = (state * vecs[1:2, lanes] + ad[:, lanes]).astype(BF16)
             backward_copy(c).start()
 
         ap[:, lanes] = (state * vecs[2:3, lanes]).astype(BF16)
 
-    first_use()
-
-    def tick(step, carry):
-        c = step - gz * HOP_STEPS
-
-        @pl.when((c >= 0) & (c < chunks))
-        def _():
-            forward_chunk(c)
-
-        @pl.when(step == LATE_STEPS)
-        def _():
-            gradients()
-
-        e = step - LATE_STEPS - (gz_count - 1 - gz) * HOP_STEPS
-
-        @pl.when((e >= 0) & (e < chunks))
-        def _():
-            backward_chunk(e)
-
-        return carry
-
-    lax.fori_loop(0, chunks + LATE_STEPS + (gz_count - 1) * HOP_STEPS, tick, 0)
-
-    def plane_chunk(c, carry):
+    @pl.when(gz == 0)
+    def _():
+        def send(c, carry):
+            sout[c] = bs[:, span(c)].astype(BF16)
+            forward_copy(c).start()
+            return carry
+
+        lax.fori_loop(0, chunks, send, 0)
+
+    product = jnp.where(lower, dot(out_map, in_map, 1, 1), 0.0)
+    mix = product.astype(BF16)
+    mix_turned = product.T.astype(BF16)
+    within[...] = dot(mix, fw[...], 1, 0)
+
+    def plane_chunk(c):
         lanes = span(c)
         pltpu.make_async_remote_copy(
             src_ref=osend.at[pl.ds(0, lat_count - 1), :, lanes],
@@ -273,10 +292,11 @@
             unroll=lat_count <= 8,
         )
         for tap in range(taps):
-            gk1[me, tap : tap + 1, lanes] = jnp.sum(sums[tap], axis=0, keepdims=True)
-        return carry
-
-    lax.fori_loop(0, chunks, plane_chunk, 0)
+            row = jnp.sum(sums[tap], axis=0, keepdims=True)
+            for tile in range(width // 128):
+                place = tap * (channels // 128) + c * (width // 128) + tile
+                gk1[me, pl.ds(place, 1), :] = row[:, tile * 128 : (tile + 1) * 128]
+
 
     def lat_start(step, carry):
         pltpu.make_async_remote_copy(
@@ -285,19 +305,10 @@
         ).start()
         return carry
 
-    lax.fori_loop(1, lat_count, lat_start, 0)
-
-    pair = jnp.where(lower, dot(gr[...], fw[...], 1, 1), 0.0)
-    gom = dot(pair.astype(BF16), in_map, 1, 0) + dot(gr[...], sp[...], 1, 1)
-    gom_ref[...] = gom.astype(BF16)
-
     lat_all = pltpu.make_async_remote_copy(
         src_ref=gk1.at[pl.ds(0, lat_count - 1)], dst_ref=gk1.at[pl.ds(0, lat_count - 1)],
         send_sem=k_sem.at[0], recv_sem=k_sem.at[1], device_id=(gz, me), device_id_type=MESH,
     )
-    lat_all.wait_recv()
-    gk2[gz] = jnp.sum(gk1[...], axis=0)
-
     def gz_start(step, carry):
         pltpu.make_async_remote_copy(
             src_ref=gk2.at[gz], dst_ref=gk2.at[gz], send_sem=k_sem.at[2], recv_sem=k_sem.at[3],
@@ -305,9 +316,56 @@
         ).start()
         return carry
 
-    lax.fori_loop(1, gz_count, gz_start, 0)
-
-    gim = dot(pair.T.astype(BF16), out_map, 1, 0) + dot(fw[...], ap[...], 1, 1)
+    def lat_begin():
+        lax.fori_loop(1, lat_count, lat_start, 0)
+        pair = jnp.where(lower, dot(gr[...], fw[...], 1, 1), 0.0)
+        gom = dot(pair.astype(BF16), in_map, 1, 0) + dot(gr[...], sp[...], 1, 1)
+        gom_ref[...] = gom.astype(BF16)
+        pair_turned[...] = pair.T.astype(BF16)
+
+    def lat_end():
+        lat_all.wait_recv()
+        gk2[gz] = jnp.sum(gk1[...], axis=0)
+
+        lax.fori_loop(1, gz_count, gz_start, 0)
+
+    def tick(step, carry):
+        c = step - gz * HOP_STEPS
+
+        @pl.when((c >= 0) & (c < chunks))
+        def _():
+            forward_chunk(c)
+
+        e = step - LATE_STEPS - (gz_count - 1 - gz) * HOP_STEPS
+
+        @pl.when(step == LATE_STEPS)
+        def _():
+            gradients()
+
+        @pl.when((e >= 0) & (e < chunks))
+        def _():
+            backward_chunk(e)
+
+        f = c - PLANE_STEPS
+
+        @pl.when((f >= 0) & (f < chunks))
+        def _():
+            plane_chunk(f)
+
+        @pl.when(f == chunks)
+        def _():
+            lat_begin()
+
+        @pl.when(f == chunks + SUM_STEPS)
+        def _():
+            lat_end()
+
+        return carry
+
+    ticks = chunks + (gz_count - 1) * HOP_STEPS + max(LATE_STEPS, PLANE_STEPS + SUM_STEPS + 1)
+    lax.fori_loop(0, ticks, tick, 0)
+
+    gim = dot(pair_turned[...], out_map, 1, 0) + dot(fw[...], ap[...], 1, 1)
     gim_ref[...] = gim.astype(BF16)
     gf = dot(mix_turned, gr[...], 1, 0) + dot(in_map, ap[...], 1, 0)
     gf_ref[...] = (wc[...] * gf + vecs[3:4, :] * grad[...]).astype(BF16)
@@ -317,7 +375,11 @@
         send_sem=k_sem.at[2], recv_sem=k_sem.at[3], device_id=(gz, me), device_id_type=MESH,
     )
     gz_all.wait_recv()
-    gk_ref[...] = jnp.sum(gk2[...], axis=0) * (1.0 / math.sqrt(row_total))
+    packed = jnp.sum(gk2[...], axis=0) * (1.0 / math.sqrt(row_total))
+    for tap in range(taps):
+        for tile in range(channels // 128):
+            place = tap * (channels // 128) + tile
+            gk_ref[tap : tap + 1, tile * 128 : (tile + 1) * 128] = packed[place : place + 1, :]
 
     lat_all.wait_send()
     gz_all.wait_send()
@@ -388,7 +450,7 @@
             pltpu.VMEM((sections, states), BF16),
             pltpu.VMEM((taps, channels), F32),
         ),
-        in_specs=[hbm, vmem, vmem, vmem, vmem, vmem, vmem, hbm],
+        in_specs=[hbm] * 8,
         out_specs=(vmem,) * 5,
         scratch_shapes=[
             pltpu.VMEM(full, BF16),
@@ -413,9 +475,16 @@
             pltpu.VMEM(turned, BF16),
             pltpu.VMEM(turned, BF16),
             pltpu.VMEM((8, channels), F32),
-            pltpu.VMEM((lat_count, taps, channels), F32),
-            pltpu.VMEM((gz_count, taps, channels), F32),
-            pltpu.SemaphoreType.DMA((2,)),
+            pltpu.VMEM((lat_count, taps * channels // 128, 128), F32),
+            pltpu.VMEM((gz_count, taps * channels // 128, 128), F32),
+            pltpu.VMEM((sections, sections), BF16),
+            pltpu.VMEM((sections, states), BF16),
+            pltpu.VMEM((sections, states), BF16),
+            pltpu.VMEM((heads, sections), F32),
+            pltpu.VMEM((1, heads), F32),
+            pltpu.VMEM((1, heads), F32),
+            pltpu.VMEM((taps, channels), F32),
+            pltpu.SemaphoreType.DMA((8,)),
             pltpu.SemaphoreType.DMA,
             pltpu.SemaphoreType.DMA,
             pltpu.SemaphoreType.DMA((chunks,)),

time: 39.9 us -> 36.3 us (0.910)
  Pallas kernels: 39 us -> 35.4 us
    pallas_call x1, Pallas kernels: 38.1 us -> 34.5 us  [per_device(): pl.pallas_call(functools.partial(kernel_body, gz_count, lat_count, width,...]
where the time goes in v3:
time: 36.3 us; the launch traced here: 36 us
  Pallas kernels  35.4 us (98%)
  between operations  0.64 us (2%)
    pallas_call x1, Pallas kernels, per_device(): pl.pallas_call(functools.partial(kernel_body, gz_count, lat_count, width,...  34.5 us
    pallas_call x1, Pallas kernels, per_device(): pl.pallas_call(write_out, out_shape=(jax.ShapeDtypeStruct(cotangent.shape...  0.94 us

profile of v3, /device:TPU:0, one launch (start us, length us, event | category | flops | bytes accessed | tf_op | source)
XLA Modules:
  0.0 36.0 jit_solution(13273504578234536699)
XLA Ops:
  0.6 34.5 %shard_map.119 = (bf16[8,16,1536]{2,1,0:T(8,128)(2,1)S(1)}, bf16[128,1536]{1,0:T(8,128)(2,1)S(1)}, bf16[128,128]{1,0:T(8,128)(2,1)S(1)}, bf16[128,128]{1,0:T(8,128)(2,1)S(1)}, f32[3,1536]{1,0:T(4,128)S(1)}) custom-call(bf16[1,128,1536]{2,1,0:T(8,128)(2,1)} %feat_hbm.1, bf16[128,128]{1,0:T(8,128)(2,1)} %bitcast.10, bf16[128,128]{1,0:T(8,128)(2,1)} %bitcast.11, ...), custom_call_target="tpu_custom_call" | custom-call | tf_op jit(solution)/shard_map/pallas_call | solution.py:444
  35.1 0.9 %shard_map.120 = (bf16[8,16,1536]{2,1,0:T(8,128)(2,1)}, bf16[128,1536]{1,0:T(8,128)(2,1)}, bf16[128,128]{1,0:T(8,128)(2,1)}, bf16[128,128]{1,0:T(8,128)(2,1)}, f32[3,1536]{1,0:T(4,128)}) custom-call(bf16[8,16,1536]{2,1,0:T(8,128)(2,1)S(1)} %get-tuple-element.15.refs_0_, bf16[128,1536]{1,0:T(8,128)(2,1)S(1)} %get-tuple-element.16.refs_1_, ...), custom_call_target="tpu_custom_call" | custom-call | tf_op jit(solution)/shard_map/pallas_call | solution.py:509

commit v4 on v3

--- a/solution.py
+++ b/solution.py
@@ -44,6 +44,8 @@
     rows = gsend.shape[1]
     taps = ker_ref.shape[0]
     chunks = channels // width
+    half = chunks // 2
+    part = half * width // 128
     aligned = rows % 16 == 0
 
     load_cot = pltpu.make_async_copy(cot_hbm, cotp.at[pl.ds(1, lat_count)], load_sem.at[0])
@@ -294,41 +296,63 @@
         for tap in range(taps):
             row = jnp.sum(sums[tap], axis=0, keepdims=True)
             for tile in range(width // 128):
-                place = tap * (channels // 128) + c * (width // 128) + tile
-                gk1[me, pl.ds(place, 1), :] = row[:, tile * 128 : (tile + 1) * 128]
-
-
-    def lat_start(step, carry):
-        pltpu.make_async_remote_copy(
-            src_ref=gk1.at[me], dst_ref=gk1.at[me], send_sem=k_sem.at[0], recv_sem=k_sem.at[1],
-            device_id=(gz, lax.rem(me + step, lat_count)), device_id_type=MESH,
-        ).start()
-        return carry
-
-    lat_all = pltpu.make_async_remote_copy(
-        src_ref=gk1.at[pl.ds(0, lat_count - 1)], dst_ref=gk1.at[pl.ds(0, lat_count - 1)],
-        send_sem=k_sem.at[0], recv_sem=k_sem.at[1], device_id=(gz, me), device_id_type=MESH,
-    )
-    def gz_start(step, carry):
-        pltpu.make_async_remote_copy(
-            src_ref=gk2.at[gz], dst_ref=gk2.at[gz], send_sem=k_sem.at[2], recv_sem=k_sem.at[3],
-            device_id=(lax.rem(gz + step, gz_count), me), device_id_type=MESH,
-        ).start()
-        return carry
-
-    def lat_begin():
-        lax.fori_loop(1, lat_count, lat_start, 0)
+                place = tap * part + lax.rem(c, half) * (width // 128) + tile
+                gk1[c // half, me, pl.ds(place, 1), :] = row[:, tile * 128 : (tile + 1) * 128]
+
+
+    def lat_start(group, dest):
+        return pltpu.make_async_remote_copy(
+            src_ref=gk1.at[group, me], dst_ref=gk1.at[group, me],
+            send_sem=k_sem.at[4 * group], recv_sem=k_sem.at[4 * group + 1],
+            device_id=(gz, dest), device_id_type=MESH,
+        )
+
+    def lat_all(group):
+        return pltpu.make_async_remote_copy(
+            src_ref=gk1.at[group, pl.ds(0, lat_count - 1)],
+            dst_ref=gk1.at[group, pl.ds(0, lat_count - 1)],
+            send_sem=k_sem.at[4 * group], recv_sem=k_sem.at[4 * group + 1],
+            device_id=(gz, me), device_id_type=MESH,
+        )
+
+    def gz_start(group, dest):
+        return pltpu.make_async_remote_copy(
+            src_ref=gk2.at[group, gz], dst_ref=gk2.at[group, gz],
+            send_sem=k_sem.at[4 * group + 2], recv_sem=k_sem.at[4 * group + 3],
+            device_id=(dest, me), device_id_type=MESH,
+        )
+
+    def gz_all(group):
+        return pltpu.make_async_remote_copy(
+            src_ref=gk2.at[group, pl.ds(0, gz_count - 1)],
+            dst_ref=gk2.at[group, pl.ds(0, gz_count - 1)],
+            send_sem=k_sem.at[4 * group + 2], recv_sem=k_sem.at[4 * group + 3],
+            device_id=(gz, me), device_id_type=MESH,
+        )
+
+    def lat_begin(group):
+        def send(step, carry):
+            lat_start(group, lax.rem(me + step, lat_count)).start()
+            return carry
+
+        lax.fori_loop(1, lat_count, send, 0)
+
+    def lat_end(group):
+        lat_all(group).wait_recv()
+        gk2[group, gz] = jnp.sum(gk1[group], axis=0)
+
+        def send(step, carry):
+            gz_start(group, lax.rem(gz + step, gz_count)).start()
+            return carry
+
+        lax.fori_loop(1, gz_count, send, 0)
+
+    def pairs():
         pair = jnp.where(lower, dot(gr[...], fw[...], 1, 1), 0.0)
         gom = dot(pair.astype(BF16), in_map, 1, 0) + dot(gr[...], sp[...], 1, 1)
         gom_ref[...] = gom.astype(BF16)
         pair_turned[...] = pair.T.astype(BF16)
 
-    def lat_end():
-        lat_all.wait_recv()
-        gk2[gz] = jnp.sum(gk1[...], axis=0)
-
-        lax.fori_loop(1, gz_count, gz_start, 0)
-
     def tick(step, carry):
         c = step - gz * HOP_STEPS
 
@@ -352,13 +376,22 @@
         def _():
             plane_chunk(f)
 
+        @pl.when(f == half)
+        def _():
+            lat_begin(0)
+
+        @pl.when(f == half + SUM_STEPS)
+        def _():
+            lat_end(0)
+
         @pl.when(f == chunks)
         def _():
-            lat_begin()
+            lat_begin(1)
+            pairs()
 
         @pl.when(f == chunks + SUM_STEPS)
         def _():
-            lat_end()
+            lat_end(1)
 
         return carry
 
@@ -370,19 +403,18 @@
     gf = dot(mix_turned, gr[...], 1, 0) + dot(in_map, ap[...], 1, 0)
     gf_ref[...] = (wc[...] * gf + vecs[3:4, :] * grad[...]).astype(BF16)
 
-    gz_all = pltpu.make_async_remote_copy(
-        src_ref=gk2.at[pl.ds(0, gz_count - 1)], dst_ref=gk2.at[pl.ds(0, gz_count - 1)],
-        send_sem=k_sem.at[2], recv_sem=k_sem.at[3], device_id=(gz, me), device_id_type=MESH,
-    )
-    gz_all.wait_recv()
-    packed = jnp.sum(gk2[...], axis=0) * (1.0 / math.sqrt(row_total))
-    for tap in range(taps):
-        for tile in range(channels // 128):
-            place = tap * (channels // 128) + tile
-            gk_ref[tap : tap + 1, tile * 128 : (tile + 1) * 128] = packed[place : place + 1, :]
-
-    lat_all.wait_send()
-    gz_all.wait_send()
+    for group in range(2):
+        gz_all(group).wait_recv()
+        packed = jnp.sum(gk2[group], axis=0) * (1.0 / math.sqrt(row_total))
+        for tap in range(taps):
+            for tile in range(part):
+                place = tap * part + tile
+                lane = (group * part + tile) * 128
+                gk_ref[tap : tap + 1, lane : lane + 128] = packed[place : place + 1, :]
+
+    for group in range(2):
+        lat_all(group).wait_send()
+        gz_all(group).wait_send()
     pltpu.make_async_remote_copy(
         src_ref=gsend.at[pl.ds(0, lat_count - 1)], dst_ref=grecv.at[pl.ds(0, lat_count - 1)],
         send_sem=gs_sem, recv_sem=gr_sem, device_id=(gz, me), device_id_type=MESH,
@@ -475,8 +507,8 @@
             pltpu.VMEM(turned, BF16),
             pltpu.VMEM(turned, BF16),
             pltpu.VMEM((8, channels), F32),
-            pltpu.VMEM((lat_count, taps * channels // 128, 128), F32),
-            pltpu.VMEM((gz_count, taps * channels // 128, 128), F32),
+            pltpu.VMEM((2, lat_count, taps * channels // 256, 128), F32),
+            pltpu.VMEM((2, gz_count, taps * channels // 256, 128), F32),
             pltpu.VMEM((sections, sections), BF16),
             pltpu.VMEM((sections, states), BF16),
             pltpu.VMEM((sections, states), BF16),
@@ -493,7 +525,7 @@
             pltpu.SemaphoreType.DMA((chunks,)),
             pltpu.SemaphoreType.DMA((chunks,)),
             pltpu.SemaphoreType.DMA((chunks,)),
-            pltpu.SemaphoreType.DMA((4,)),
+            pltpu.SemaphoreType.DMA((8,)),
         ],
         compiler_params=pltpu.CompilerParams(collective_id=0, has_side_effects=True),
     )(

time: 36.3 us -> 37.9 us (1.044)
  Pallas kernels: 35.4 us -> 37 us
    pallas_call x1, Pallas kernels: 34.5 us -> 36.1 us  [per_device(): pl.pallas_call(functools.partial(kernel_body, gz_count, lat_count, width,...]
where the time goes in v4:
time: 37.9 us; the launch traced here: 37.7 us
  Pallas kernels  37 us (98%)
  between operations  0.64 us (2%)
    pallas_call x1, Pallas kernels, per_device(): pl.pallas_call(functools.partial(kernel_body, gz_count, lat_count, width,...  36.1 us
    pallas_call x1, Pallas kernels, per_device(): pl.pallas_call(write_out, out_shape=(jax.ShapeDtypeStruct(cotangent.shape...  0.94 us

profile of v4, /device:TPU:0, one launch (start us, length us, event | category | flops | bytes accessed | tf_op | source)
XLA Modules:
  0.0 37.7 jit_solution(10732496054706608518)
XLA Ops:
  0.6 36.1 %shard_map.119 = (bf16[8,16,1536]{2,1,0:T(8,128)(2,1)S(1)}, bf16[128,1536]{1,0:T(8,128)(2,1)S(1)}, bf16[128,128]{1,0:T(8,128)(2,1)S(1)}, bf16[128,128]{1,0:T(8,128)(2,1)S(1)}, f32[3,1536]{1,0:T(4,128)S(1)}) custom-call(bf16[1,128,1536]{2,1,0:T(8,128)(2,1)} %feat_hbm.1, bf16[128,128]{1,0:T(8,128)(2,1)} %bitcast.10, bf16[128,128]{1,0:T(8,128)(2,1)} %bitcast.11, ...), custom_call_target="tpu_custom_call" | custom-call | tf_op jit(solution)/shard_map/pallas_call | solution.py:476
  36.7 0.9 %shard_map.120 = (bf16[8,16,1536]{2,1,0:T(8,128)(2,1)}, bf16[128,1536]{1,0:T(8,128)(2,1)}, bf16[128,128]{1,0:T(8,128)(2,1)}, bf16[128,128]{1,0:T(8,128)(2,1)}, f32[3,1536]{1,0:T(4,128)}) custom-call(bf16[8,16,1536]{2,1,0:T(8,128)(2,1)S(1)} %get-tuple-element.15.refs_0_, bf16[128,1536]{1,0:T(8,128)(2,1)S(1)} %get-tuple-element.16.refs_1_, ...), custom_call_target="tpu_custom_call" | custom-call | tf_op jit(solution)/shard_map/pallas_call | solution.py:541
